TPU v7x, 128 devices: a whole 4x4x4 slice. The times are simulated.
128 devices in a mesh: row: 16 (over z, y), col: 8 (over x, core).
Axes of the slice: x: 4, y: 4, z: 4, core: 2. Of those that a mesh axis runs over, the one named last changes fastest.
Arguments:
- trailing: float32 [16384, 16384], P('row', 'col'), may hold values from -40 to 40, as said below
- factor_one: float32 [16384, 512], P(('row', 'col')), may hold values from -0.0390625 to 0.0390625
- inverse_one: float32 [512, 512], replicated, may hold values from -1 to 2, as said below
- factor_two_top: float32 [512, 512], replicated, may hold values from -0.0390625 to 0.0390625
- factor_two: float32 [16384, 512], P(('row', 'col')), may hold values from -0.0390625 to 0.0390625
- inverse_two: float32 [512, 512], replicated, may hold values from -1 to 2, as said below
- structure_one: int32 [96], replicated, may hold values from 0 to 127, as said below
- structure_two: int32 [94], replicated, may hold values from 0 to 127, as said below
Outputs:
- column_one: float32 [16384, 512], P(('row', 'col'))
- diagonal_one: float32 [512, 512], replicated
- column_two: float32 [16384, 512], P(('row', 'col'))
- cross_two: float32 [512, 512], replicated
- diagonal_two: float32 [512, 512], replicated
Inputs may be any that keep to these rules, and one draw needn't show every extreme that they name: `trailing`: symmetric. `inverse_one`: lower triangular, diagonal between 1 and 2. `inverse_two`: lower triangular, diagonal between 1 and 2. `structure_one`: distinct, rising; lists block 0 and the last block. `structure_two`: distinct, rising, each also listed in structure_one; lists block 0 and the last block.
All inputs are finite; a program needn't handle non-finite values.
Results may differ from a plain program's by a relative error of at most 0.0003.
Values sent between devices are 32-bit elements; how exact they have to be, the bound alone decides.
No kernel may reach another device: no remote copies, remote signals or barrier semaphores. Data moves between devices by JAX's collectives and lax.ppermute only.
A program may use at most 128 MiB of HBM per device.

v0:
```python
import jax
import jax.numpy as jnp
from jax import lax
from jax.sharding import PartitionSpec as P

BLK = 128


def spread(x, axis, root):
    mine = lax.axis_index(axis) == root
    return lax.psum(jnp.where(mine, x, jnp.zeros_like(x)), axis)


def product(left, right):
    return jnp.dot(left, right, precision=lax.Precision.HIGHEST, preferred_element_type=jnp.float32)


def block_flags(structure, first_row, count):
    blocks = (first_row + jnp.arange(count, dtype=jnp.int32)) // BLK
    hits = jnp.any(blocks[:, None] == structure[None, :], axis=1)
    return hits.astype(jnp.float32)[:, None]


def panel_apart(normal, col_index, spread_count):
    row_block = lax.all_gather(normal, "col", axis=0, tiled=True)
    pieces = []
    for offset in range(spread_count):
        pieces.append(spread(row_block, "row", col_index * spread_count + offset))
    return (row_block, jnp.concatenate(pieces, axis=0))


def sweep(trailing, col_block, own_normal):
    summed = lax.psum_scatter(-product(trailing, col_block), "col", scatter_dimension=0, tiled=True)
    quad_part = product(own_normal.T, summed)
    return (summed, quad_part)


def body(
    trailing,
    factor_one,
    inverse_one,
    factor_two_top,
    factor_two,
    inverse_two,
    structure_one,
    structure_two,
):
    piece_rows = factor_one.shape[0]
    spread_count = lax.axis_size("row") // lax.axis_size("col")
    row_index = lax.axis_index("row")
    col_index = lax.axis_index("col")
    first_row = (row_index * lax.axis_size("col") + col_index) * piece_rows
    mask_one = block_flags(structure_one, first_row, piece_rows)
    mask_two = block_flags(structure_two, first_row, piece_rows)
    normal_one = mask_one * product(factor_one, inverse_one)
    normal_two = mask_two * product(factor_two, inverse_two)
    rows_one, cols_one = panel_apart(normal_one, col_index, spread_count)
    rows_two, cols_two = panel_apart(normal_two, col_index, spread_count)
    summed_one, quad_one = sweep(trailing, cols_one, normal_one)
    column_one = mask_one * summed_one
    diag_total = lax.psum(quad_one, ("row", "col"))
    diagonal_one = product(inverse_one.T, inverse_one) - diag_total
    normal_top = product(factor_two_top, inverse_two)
    summed_two, quad_two = sweep(trailing, cols_two, normal_two)
    local_part = -product(column_one, normal_top)
    column_two = mask_two * (local_part + summed_two)
    cross_total, second_total = lax.psum(
        (product(column_one.T, normal_two), product(normal_two.T, local_part) + quad_two),
        ("row", "col"),
    )
    cross_two = -(product(diagonal_one, normal_top) + cross_total)
    diagonal_two = (
        product(inverse_two.T, inverse_two) - product(normal_top.T, cross_two) - second_total
    )
    return (column_one, diagonal_one, column_two, cross_two, diagonal_two)


def solution(mesh):
    return jax.shard_map(
        body,
        mesh=mesh,
        in_specs=(
            P("row", "col"),
            P(("row", "col"), None),
            P(),
            P(),
            P(("row", "col"), None),
            P(),
            P(),
            P(),
        ),
        out_specs=(P(("row", "col"), None), P(), P(("row", "col"), None), P(), P()),
        check_vma=False,
    )
```

profile of v0, /device:TPU:1, one launch (start us, length us, event | category | flops | bytes accessed | tf_op | source)
XLA Modules:
  0.0 474.7 jit_solution(2318638378639296707)
XLA Ops:
  7.3 0.9 compare_reduce_fusion
  8.4 2.4 convolution_multiply_fusion
  11.6 2.4 convolution_multiply_fusion.1
  14.1 25.6 %all-gather.5.cloned.1.call-done = f32[1024,512]{1,0:T(8,128)} async-done(((f32[128,512]{1,0:T(8,128)}), f32[1024,512]{1,0:T(8,128)}) %all-gather.5.cloned.1.call-update) | async-done | bytes 2097168 | tf_op jit(solution)/shard_map/all_gather | solution.py:25
  39.7 4.2 broadcast_select_fusion.1
  43.9 23.5 %all-gather.3.cloned.1.call-done = f32[1024,512]{1,0:T(8,128)} async-done(((f32[128,512]{1,0:T(8,128)}), f32[1024,512]{1,0:T(8,128)}) %all-gather.3.cloned.1.call-update) | async-done | bytes 2097168 | tf_op jit(solution)/shard_map/all_gather | solution.py:25
  67.5 4.2 broadcast_select_fusion.3
  71.7 142.3 %all-reduce.7.cloned.1.call-done = (f32[1024,512]{1,0:T(8,128)}, f32[1024,512]{1,0:T(8,128)}, f32[1024,512]{1,0:T(8,128)}, f32[1024,512]{1,0:T(8,128)}) async-done(((f32[1024,512]{1,0:T(8,128)}, f32[1024,512]{1,0:T(8,128)}, f32[1024,512]{1,0:T(8,128)}, f32[1024,512]{1,0:T(8,128)}), (f32[1024,512]{1,0:T(8,128)}, f32[1024,512]{1,0:T(8,128)}, f32[1024,512]{1,0:T(8,128)}, ...) | async-done | bytes 8388624 | tf_op jit(solution)/shard_map/psum | solution.py:11
  214.0 17.6 %negate_bitcast_fusion.1 = f32[1024,512]{1,0:T(8,128)} fusion(f32[1024,2048]{1,0:T(8,128)} %param.8, f32[1024,512]{1,0:T(8,128)} %get-tuple-element.8, f32[1024,512]{1,0:T(8,128)} %get-tuple-element.9), kind=kOutput, calls=%fused_computation.9 | convolution fusion | flops 12886474752 | bytes 14680064 | tf_op jit(solution)/shard_map/dot_general | solution.py:15
  231.8 17.7 %negate_bitcast_fusion = f32[1024,512]{1,0:T(8,128)} fusion(f32[1024,2048]{1,0:T(8,128)} %param.8, f32[1024,512]{1,0:T(8,128)} %get-tuple-element.10, f32[1024,512]{1,0:T(8,128)} %get-tuple-element.11), kind=kOutput, calls=%fused_computation.8 | convolution fusion | flops 12886474752 | bytes 14680064 | tf_op jit(solution)/shard_map/dot_general | solution.py:15
  249.7 3.1 fusion.17
  252.8 9.0 %reduce-scatter.3.cloned.1.call-done = f32[128,512]{1,0:T(8,128)} async-done(((f32[1024,512]{1,0:T(8,128)}), f32[128,512]{1,0:T(8,128)}) %reduce-scatter.3.cloned.1.call-update) | async-done | bytes 262160 | tf_op jit(solution)/shard_map/reduce_scatter | solution.py:33
  261.8 1.0 broadcast_multiply_fusion
  263.6 2.0 fusion.18
  265.6 31.1 %reduce-scatter.5.cloned.1.call-done = f32[128,512]{1,0:T(8,128)} async-done(((f32[1024,512]{1,0:T(8,128)}), f32[128,512]{1,0:T(8,128)}) %reduce-scatter.5.cloned.1.call-update) | async-done | bytes 262160 | tf_op jit(solution)/shard_map/reduce_scatter | solution.py:33
  296.7 2.5 add_multiply_fusion
  299.2 1.0 fusion.20
  300.3 2.0 fusion.16
  302.3 2.0 convolution_add_fusion.1
  304.3 2.9 fusion.19
  307.2 152.7 %all-reduce.5.cloned.1.call-done = (f32[512,512]{1,0:T(8,128)}, f32[512,512]{1,0:T(8,128)}, f32[512,512]{1,0:T(8,128)}) async-done(((f32[512,512]{1,0:T(8,128)}, f32[512,512]{1,0:T(8,128)}, f32[512,512]{1,0:T(8,128)}), (f32[512,512]{1,0:T(8,128)}, f32[512,512]{1,0:T(8,128)}, f32[512,512]{1,0:T(8,128)})) %all-reduce.5.cloned.1.call-update) | async-done | bytes 3145744 | tf_op jit(solution)/shard_map/psum | solution.py:61
  459.8 3.2 convolution_subtract_fusion.1
  463.1 1.9 fusion.13
  465.0 2.9 fusion.12
  (40 shorter events, 2.3 us)
Async XLA Ops:
  7.2 1.2 copy-start
  7.2 4.4 copy-start.1
  7.2 32.5 %all-gather.5.cloned.1.call-start = ((), (), s32[]{:S(2)}) async-start(), calls=%async_computation.4 | async-start | bytes 2359296 | tf_op jit(solution)/shard_map/all_gather | solution.py:25
  10.8 56.7 %all-gather.3.cloned.1.call-start = ((), (), s32[]{:S(2)}) async-start(), calls=%async_computation.2 | async-start | bytes 2359296 | tf_op jit(solution)/shard_map/all_gather | solution.py:25
  14.0 200.0 %all-reduce.7.cloned.1.call-start = ((), (), s32[]{:S(2)}) async-start(), calls=%async_computation.7 | async-start | bytes 16777216 | tf_op jit(solution)/shard_map/psum | solution.py:11
  71.7 190.2 %reduce-scatter.3.cloned.1.call-start = ((), (), s32[]{:S(2)}) async-start(), calls=%async_computation.3 | async-start | bytes 2359296 | tf_op jit(solution)/shard_map/reduce_scatter | solution.py:33
  231.7 65.0 %reduce-scatter.5.cloned.1.call-start = ((), (), s32[]{:S(2)}) async-start(), calls=%async_computation.5 | async-start | bytes 2359296 | tf_op jit(solution)/shard_map/reduce_scatter | solution.py:33
  249.5 14.1 %copy-start.2 = (f32[128,512]{1,0:T(8,128)S(1)}, f32[128,512]{1,0:T(8,128)}, u32[]{:S(2)}) copy-start(f32[128,512]{1,0:T(8,128)} %convolution_multiply_fusion) | copy-start | bytes 786436
  249.5 210.4 %all-reduce.5.cloned.1.call-start = ((), (), s32[]{:S(2)}) async-start(), calls=%async_computation.6 | async-start | bytes 6291456 | tf_op jit(solution)/shard_map/psum | solution.py:61
  262.9 0.7 copy-start.6
  296.7 3.6 copy-start.7
  296.7 3.6 copy-start.10
  299.2 3.1 copy-start.9
  459.8 3.2 copy-start.11
  463.0 1.9 copy-start.5
  463.0 1.9 copy-start.3
  463.1 1.9 copy-start.8
  464.9 2.9 copy-start.4
Sparse Core Ops, SparseCore 0:
  10.9 28.7 all-gather.4
  42.0 25.4 all-gather.2
  71.8 142.2 all-reduce.6
  231.8 29.9 reduce-scatter.2
  264.2 32.4 reduce-scatter.4
  304.5 155.3 all-reduce.4
where the time goes:
time: 475 us
  waiting for transfers between devices  384 us (81%)
  matrix products  63.5 us (13%)
  between operations  14.3 us (3%)
  other arithmetic  11.1 us (2%)
    psum x1, waiting for transfers between devices, body(): diag_total = lax.psum(quad_one, ('row', 'col'))  153 us
    psum x1, waiting for transfers between devices, spread(): return lax.psum(jnp.where(mine, x, jnp.zeros_like(x)), axis)  142 us
    dot_general x14, matrix products, product(): jnp.dot(left, right, precision=lax.Precision.HIGHEST, preferred_element_t...  63.5 us
    all_gather x2, waiting for transfers between devices, panel_apart(): row_block = lax.all_gather(normal, 'col', axis=0, tiled=True)  49.2 us
    reduce_scatter x2, waiting for transfers between devices, sweep(): lax.psum_scatter(-product(trailing, col_block), 'col', scatter_dimension=...  40.2 us
  transfers between devices with their start and end apart: 6, of which 6 were waited for; matrix products, arithmetic and copies ran while one was open for 7% of the time, Pallas kernels for 0%

commit v1 on v0

--- a/solution.py
+++ b/solution.py
@@ -58,7 +58,7 @@
     rows_two, cols_two = panel_apart(normal_two, col_index, spread_count)
     summed_one, quad_one = sweep(trailing, cols_one, normal_one)
     column_one = mask_one * summed_one
-    diag_total = lax.psum(quad_one, ("row", "col"))
+    diag_total = lax.psum(lax.psum(quad_one, "col"), "row")
     diagonal_one = product(inverse_one.T, inverse_one) - diag_total
     normal_top = product(factor_two_top, inverse_two)
     summed_two, quad_two = sweep(trailing, cols_two, normal_two)

time: 475 us -> 627 us (1.32)
  waiting for transfers between devices: 384 us -> 538 us
    psum x1 -> x3, waiting for transfers between devices: 153 us -> 326 us  [the longest x2 177 us: body(): diag_total = lax.psum(lax.psum(quad_one, 'col'), 'row')]
    psum x1, waiting for transfers between devices: 142 us -> 104 us  [spread(): return lax.psum(jnp.where(mine, x, jnp.zeros_like(x)), axis)]
    reduce_scatter x2, waiting for transfers between devices: 40.2 us -> 53.5 us  [sweep(): lax.psum_scatter(-product(trailing, col_block), 'col', scatter_dimension=...]
  transfers between devices with their start and end apart: 6 -> 8, of which waited for: 6 -> 8; matrix products, arithmetic and copies ran while one was open for 7% -> 3% of each run, Pallas kernels for 0% -> 0%
where the time goes in v1:
time: 627 us
  waiting for transfers between devices  538 us (86%)
  matrix products  62.8 us (10%)
  between operations  14.3 us (2%)
  other arithmetic  9.5 us (2%)
    psum x2, waiting for transfers between devices, body(): diag_total = lax.psum(lax.psum(quad_one, 'col'), 'row')  177 us
    psum x1, waiting for transfers between devices, body(): lax.psum((product(column_one.T, normal_two), product(normal_two.T, local_...  149 us
    psum x1, waiting for transfers between devices, spread(): return lax.psum(jnp.where(mine, x, jnp.zeros_like(x)), axis)  104 us
    dot_general x14, matrix products, product(): jnp.dot(left, right, precision=lax.Precision.HIGHEST, preferred_element_t...  62.8 us
    all_gather x2, waiting for transfers between devices, panel_apart(): row_block = lax.all_gather(normal, 'col', axis=0, tiled=True)  55.2 us
    reduce_scatter x2, waiting for transfers between devices, sweep(): lax.psum_scatter(-product(trailing, col_block), 'col', scatter_dimension=...  53.5 us
  transfers between devices with their start and end apart: 8, of which 8 were waited for; matrix products, arithmetic and copies ran while one was open for 3% of the time, Pallas kernels for 0%

profile of v1, /device:TPU:1, one launch (start us, length us, event | category | flops | bytes accessed | tf_op | source)
XLA Modules:
  0.0 627.1 jit_solution(274406606482709743)
XLA Ops:
  8.1 2.7 convolution_multiply_fusion.1
  10.9 28.8 %all-gather.3.cloned.1.call-done = f32[1024,512]{1,0:T(8,128)} async-done(((f32[128,512]{1,0:T(8,128)}), f32[1024,512]{1,0:T(8,128)}) %all-gather.3.cloned.1.call-update) | async-done | bytes 2097168 | tf_op jit(solution)/shard_map/all_gather | solution.py:25
  39.8 4.2 broadcast_select_fusion.3
  44.1 103.6 %all-reduce.14.cloned.1.call-done = (f32[1024,512]{1,0:T(8,128)}, f32[1024,512]{1,0:T(8,128)}) async-done(((f32[1024,512]{1,0:T(8,128)}, f32[1024,512]{1,0:T(8,128)}), (f32[1024,512]{1,0:T(8,128)}, f32[1024,512]{1,0:T(8,128)})) %all-reduce.14.cloned.1.call-update) | async-done | bytes 4194320 | tf_op jit(solution)/shard_map/psum | solution.py:11
  147.7 17.6 %negate_bitcast_fusion.1 = f32[1024,512]{1,0:T(8,128)} fusion(f32[1024,2048]{1,0:T(8,128)} %param.8, f32[1024,512]{1,0:T(8,128)} %get-tuple-element.10, f32[1024,512]{1,0:T(8,128)} %get-tuple-element.11), kind=kOutput, calls=%fused_computation.9 | convolution fusion | flops 12886474752 | bytes 14680064 | tf_op jit(solution)/shard_map/dot_general | solution.py:15
  166.3 1.4 convolution_multiply_fusion
  167.8 28.3 %reduce-scatter.3.cloned.1.call-done = f32[128,512]{1,0:T(8,128)} async-done(((f32[1024,512]{1,0:T(8,128)}), f32[128,512]{1,0:T(8,128)}) %reduce-scatter.3.cloned.1.call-update) | async-done | bytes 262160 | tf_op jit(solution)/shard_map/reduce_scatter | solution.py:33
  196.1 2.9 fusion.16
  199.1 26.4 %all-gather.5.cloned.1.call-done = f32[1024,512]{1,0:T(8,128)} async-done(((f32[128,512]{1,0:T(8,128)}), f32[1024,512]{1,0:T(8,128)}) %all-gather.5.cloned.1.call-update) | async-done | bytes 2097168 | tf_op jit(solution)/shard_map/all_gather | solution.py:25
  225.5 4.2 broadcast_select_fusion.1
  229.7 58.8 %all-reduce.8.cloned.1.call-done = f32[512,512]{1,0:T(8,128)} async-done(((f32[512,512]{1,0:T(8,128)}), f32[512,512]{1,0:T(8,128)}) %all-reduce.8.cloned.1.call-update) | async-done | bytes 1048592 | tf_op jit(solution)/shard_map/psum | solution.py:61
  288.6 118.3 %all-reduce.12.cloned.1.call-done = (f32[512,512]{1,0:T(8,128)}, f32[1024,512]{1,0:T(8,128)}, f32[1024,512]{1,0:T(8,128)}) async-done(((f32[512,512]{1,0:T(8,128)}, f32[1024,512]{1,0:T(8,128)}, f32[1024,512]{1,0:T(8,128)}), (f32[512,512]{1,0:T(8,128)}, f32[1024,512]{1,0:T(8,128)}, f32[1024,512]{1,0:T(8,128)})) %all-reduce.12.cloned.1.call-update) | async-done | bytes 5242896 | tf_op jit(solution)/shard_map/psum | solution.py:61
  406.9 17.6 %negate_bitcast_fusion = f32[1024,512]{1,0:T(8,128)} fusion(f32[1024,2048]{1,0:T(8,128)} %param.8, f32[1024,512]{1,0:T(8,128)} %get-tuple-element.8, f32[1024,512]{1,0:T(8,128)} %get-tuple-element.9), kind=kOutput, calls=%fused_computation.8 | convolution fusion | flops 12886474752 | bytes 14680064 | tf_op jit(solution)/shard_map/dot_general | solution.py:15
  425.7 1.8 fusion.17
  427.7 2.0 fusion.18
  429.7 25.3 %reduce-scatter.5.cloned.1.call-done = f32[128,512]{1,0:T(8,128)} async-done(((f32[1024,512]{1,0:T(8,128)}), f32[128,512]{1,0:T(8,128)}) %reduce-scatter.5.cloned.1.call-update) | async-done | bytes 262160 | tf_op jit(solution)/shard_map/reduce_scatter | solution.py:33
  455.0 2.4 add_multiply_fusion
  457.4 1.0 fusion.20
  458.5 2.0 convolution_add_fusion.1
  460.5 1.9 fusion.19
  462.4 2.8 convolution_subtract_fusion.1
  465.2 148.5 %all-reduce.10.cloned.1.call-done = (f32[512,512]{1,0:T(8,128)}, f32[512,512]{1,0:T(8,128)}) async-done(((f32[512,512]{1,0:T(8,128)}, f32[512,512]{1,0:T(8,128)}), (f32[512,512]{1,0:T(8,128)}, f32[512,512]{1,0:T(8,128)})) %all-reduce.10.cloned.1.call-update) | async-done | bytes 2097168 | tf_op jit(solution)/shard_map/psum | solution.py:67
  613.8 3.5 fusion.13
  617.3 2.9 fusion.12
  (48 shorter events, 3.4 us)
Async XLA Ops:
  7.2 158.9 %copy-start = (f32[512,512]{1,0:T(8,128)S(1)}, f32[512,512]{1,0:T(8,128)}, u32[]{:S(2)}) copy-start(f32[512,512]{1,0:T(8,128)} %param.13) | copy-start | bytes 3145732
  7.2 32.6 %all-gather.3.cloned.1.call-start = ((), (), s32[]{:S(2)}) async-start(), calls=%async_computation.2 | async-start | bytes 2359296 | tf_op jit(solution)/shard_map/all_gather | solution.py:25
  10.8 136.8 %all-reduce.14.cloned.1.call-start = ((), (), s32[]{:S(2)}) async-start(), calls=%async_computation.9 | async-start | bytes 8388608 | tf_op jit(solution)/shard_map/psum | solution.py:11
  44.0 152.1 %reduce-scatter.3.cloned.1.call-start = ((), (), s32[]{:S(2)}) async-start(), calls=%async_computation.3 | async-start | bytes 2359296 | tf_op jit(solution)/shard_map/reduce_scatter | solution.py:33
  165.3 0.7 copy-start.12
  165.3 1.0 copy-start.11
  165.3 30.8 %copy-start.5 = (f32[128,512]{1,0:T(8,128)S(1)}, f32[128,512]{1,0:T(8,128)}, u32[]{:S(2)}) copy-start(f32[128,512]{1,0:T(8,128)} %convolution_multiply_fusion.1) | copy-start | bytes 786436
  165.3 60.1 %all-gather.5.cloned.1.call-start = ((), (), s32[]{:S(2)}) async-start(), calls=%async_computation.5 | async-start | bytes 2359296 | tf_op jit(solution)/shard_map/all_gather | solution.py:25
  167.7 120.8 %all-reduce.8.cloned.1.call-start = ((), (), s32[]{:S(2)}) async-start(), calls=%async_computation.4 | async-start | bytes 2097152 | tf_op jit(solution)/shard_map/psum | solution.py:61
  199.0 207.8 %all-reduce.12.cloned.1.call-start = ((), (), s32[]{:S(2)}) async-start(), calls=%async_computation.8 | async-start | bytes 10485760 | tf_op jit(solution)/shard_map/psum | solution.py:61
  288.5 166.4 %reduce-scatter.5.cloned.1.call-start = ((), (), s32[]{:S(2)}) async-start(), calls=%async_computation.6 | async-start | bytes 2359296 | tf_op jit(solution)/shard_map/reduce_scatter | solution.py:33
  424.5 1.2 copy-start.6
  424.5 3.2 copy-start.2
  424.5 189.2 %all-reduce.10.cloned.1.call-start = ((), (), s32[]{:S(2)}) async-start(), calls=%async_computation.7 | async-start | bytes 4194304 | tf_op jit(solution)/shard_map/psum | solution.py:67
  425.7 1.9 copy-start.9
  427.7 30.7 %copy-start.4 = (f32[128,512]{1,0:T(8,128)}, f32[128,512]{1,0:T(8,128)S(1)}, u32[]{:S(2)}) copy-start(f32[128,512]{1,0:T(8,128)S(1)} %broadcast_multiply_fusion) | copy-start | bytes 786436
  455.0 3.5 copy-start.8
  460.5 1.9 copy-start.1
  460.5 1.9 copy-start.10
  613.8 3.6 copy-start.7
  617.3 3.0 copy-start.3
Sparse Core Ops, SparseCore 0:
  11.0 28.7 all-gather.2
  44.1 103.4 all-reduce.13
  165.5 30.5 reduce-scatter.2
  198.2 27.2 all-gather.4
  228.2 60.2 all-reduce.7
  292.1 114.7 all-reduce.11
  424.6 30.2 reduce-scatter.4
  461.4 152.3 all-reduce.9
